TPU v7x, 128 devices: a whole 4x4x4 slice. The times are simulated.
128 devices in a mesh: row: 8 (over x, core), col: 16 (over z, y).
Axes of the slice: x: 4, y: 4, z: 4, core: 2. Of those that a mesh axis runs over, the one named last changes fastest.
Arguments:
- hamiltonian: float32 [256, 4, 128, 128], P(('row', 'col')), may hold values from -20 to 20
- block_lists: int32 [256, 4], replicated, may hold values from -1 to 255, as said below
Outputs:
- density: float32 [256, 4, 128, 128], P(('row', 'col'))
Inputs may be any that keep to these rules, and one draw needn't show every extreme that they name: `block_lists`: block column j = (r * 16 + c) * 2 + s sits on grid row r, grid column c, slot s. Entry 0 is j. Entry 1 is the column of the same r and s at grid column c - 1 (cyclically), entry 2 the one at c + 1, each either present or -1, present for both ends of a link or for neither. Entry 3 is never -1: the column of the same c and s on grid row r with one bit flipped, the same bit for all rows of one grid column and slot. Some columns have all four entries, some only entries 0 and 3.
All inputs are finite; a program needn't handle non-finite values.
Results may differ from a plain program's by a relative error of at most 0.0001.
Values sent between devices are 32-bit elements; how exact they have to be, the bound alone decides.
A program may use at most 64 MiB of HBM per device.

v0:
```python
import jax
import jax.numpy as jnp
from jax import lax
from jax.sharding import PartitionSpec as P

ITERS = 6
STEPS = 2
epsilon = 1e-06


def with_halo(block, sides, width):
    for axis, dim in sides:
        count = lax.axis_size(axis)
        forward = [(i, i + 1) for i in range(count - 1)]
        forward.append((count - 1, 0))
        backward = [(target, source) for source, target in forward]
        low = lax.ppermute(
            lax.slice_in_dim(block, block.shape[dim] - width, None, axis=dim), axis, forward
        )
        high = lax.ppermute(lax.slice_in_dim(block, 0, width, axis=dim), axis, backward)
        block = jnp.concatenate([low, block, high], axis=dim)
    return block


def symmetric(matrix):
    return 0.5 * (matrix + jnp.swapaxes(matrix, -1, -2))


def assemble(own_col, diagonals, face_blocks, present):
    column = 0.5 * (own_col + jnp.swapaxes(face_blocks, -1, -2)) * present[:, None, None]
    blocks = symmetric(diagonals) * present[:, None, None]
    side_len = own_col.shape[-1]
    members = own_col.shape[0]
    matrix = jnp.zeros((members, side_len, members, side_len), jnp.float32)
    matrix = matrix.at[0, :, 0, :].set(column[0])
    for position in range(1, members):
        matrix = matrix.at[position, :, 0, :].set(column[position])
        matrix = matrix.at[0, :, position, :].set(column[position].T)
        matrix = matrix.at[position, :, position, :].set(blocks[position])
    return matrix.reshape(members * side_len, members * side_len)


def sign_batch(matrices, first_squares, scaling, present):
    slots_here = matrices.shape[0]
    full_order = matrices.shape[1]
    members = present.shape[1]
    side_len = full_order // members
    identity = jnp.eye(full_order, dtype=jnp.float32)
    iterate = matrices * scaling
    square = first_squares * (scaling * scaling)
    for repeat in range(ITERS):
        if repeat > 0:
            square = jnp.einsum("sab,sbc->sac", iterate, iterate, precision=lax.Precision.HIGHEST)
        iterate = jnp.einsum(
            "sab,sbc->sac", iterate, 1.5 * identity - 0.5 * square, precision=lax.Precision.HIGHEST
        )
    central = 0.5 * (identity[:, :side_len] - iterate[:, :, :side_len])
    return central.reshape(slots_here, members, side_len, side_len) * present[:, :, None, None]


def per_device(hamiltonian, block_lists):
    slots_here = hamiltonian.shape[0]
    cycle_size = lax.axis_size("col")
    my_row = lax.axis_index("row")
    device = my_row * cycle_size + lax.axis_index("col")
    my_lists = lax.dynamic_slice_in_dim(block_lists, device * slots_here, slots_here, 0)
    present = (my_lists >= 0).astype(jnp.float32)
    partner_row = my_lists[:, 3] // slots_here // cycle_size
    slot_ids = jnp.arange(slots_here, dtype=jnp.int32)
    cycle_cols = with_halo(hamiltonian[None], (("col", 0),), 1)
    stored_left_diag = cycle_cols[0][:, 0]
    stored_left_face = cycle_cols[0][:, 2]
    stored_right_diag = cycle_cols[2][:, 0]
    stored_right_face = cycle_cols[2][:, 1]
    partner_pos = 3
    everyone = lax.all_gather(hamiltonian[None], "row", axis=0, tiled=True)
    partner = everyone[partner_row, slot_ids]
    stored_part_diag = partner[:, 0]
    stored_part_face = partner[:, partner_pos]
    left_diag, left_face = (stored_left_diag, stored_left_face)
    right_diag, right_face = (stored_right_diag, stored_right_face)
    part_diag, part_face = (stored_part_diag, stored_part_face)
    current = hamiltonian
    density = hamiltonian
    for scf_round in range(STEPS):
        diagonals = jnp.stack((current[:, 0], left_diag, right_diag, part_diag), 1)
        face_blocks = jnp.stack((current[:, 0], left_face, right_face, part_face), 1)
        matrices = jax.vmap(assemble)(current, diagonals, face_blocks, present)
        first_squares = jnp.einsum(
            "sab,sbc->sac", matrices, matrices, precision=lax.Precision.HIGHEST
        )
        local_top = jnp.max(jnp.sum(first_squares * first_squares, axis=(1, 2)))
        largest = lax.pmax(local_top, ("row", "col"))
        scaling = 1.5 / jnp.sqrt(jnp.sqrt(largest + epsilon))
        density_cols = sign_batch(matrices, first_squares, scaling, present)
        cycle_dens = with_halo(density_cols[None], (("col", 0),), 1)
        left_dens = cycle_dens[0][:, 2]
        left_centre = cycle_dens[0][:, 0]
        right_dens = cycle_dens[2][:, 1]
        right_centre = cycle_dens[2][:, 0]
        sent_partner = jnp.stack((density_cols[:, 3], density_cols[:, 0]), 1)
        everyone_dens = lax.all_gather(sent_partner[None], "row", axis=0, tiled=True)
        partner_pair = everyone_dens[partner_row, slot_ids]
        partner_dens = partner_pair[:, 0]
        partner_centre = partner_pair[:, 1]
        density_face = jnp.stack((density_cols[:, 0], left_dens, right_dens, partner_dens), 1)
        density = (
            0.5 * (density_cols + jnp.swapaxes(density_face, -1, -2)) * present[:, :, None, None]
        )
        if scf_round + 1 < STEPS:
            current = hamiltonian + density
            density_turned = jnp.swapaxes(density, -1, -2)
            left_diag = stored_left_diag + symmetric(left_centre)
            right_diag = stored_right_diag + symmetric(right_centre)
            part_diag = stored_part_diag + symmetric(partner_centre)
            left_face = stored_left_face + density_turned[:, 1]
            right_face = stored_right_face + density_turned[:, 2]
            part_face = stored_part_face + density_turned[:, 3]
    return density


def solution(mesh):
    return jax.shard_map(
        per_device,
        mesh=mesh,
        in_specs=(P(("row", "col"), None, None, None), P()),
        out_specs=P(("row", "col"), None, None, None),
        check_vma=False,
    )
```

profile of v0, /device:TPU:1, one launch (start us, length us, event | category | flops | bytes accessed | tf_op | source)
XLA Modules:
  0.0 403.3 jit_solution(2100939602717630604)
XLA Ops:
  8.6 2.2 collective-permute-start
  10.7 5.0 %collective-permute-start.1 = (f32[1,2,4,128,128]{3,4,1,2,0:T(8,128)S(1)}, f32[1,2,4,128,128]{3,4,1,2,0:T(8,128)}, u32[]{:S(2)}, u32[]{:S(2)}) collective-permute-start(f32[1,2,4,128,128]{3,4,1,2,0:T(8,128)S(1)} %bitcast.234), channel_id=1, source_target_pairs={{1,0},{2,1},{3,2},{4,3},{5,4},{6,5},{7,6},{8,7},{9,8},{10,9},{11,1... | collective-permute-start | bytes 1572872 | tf_op jit(solution)/shard_map/ppermute | solution.py:20
  18.6 1.3 concatenate.53
  19.9 1.5 concatenate.54
  22.9 4.3 %collective-permute-done = f32[1,2,4,128,128]{3,4,1,2,0:T(8,128)S(1)} collective-permute-done((f32[1,2,4,128,128]{3,4,1,2,0:T(8,128)S(1)}, f32[1,2,4,128,128]{3,4,1,2,0:T(8,128)S(1)}, u32[]{:S(2)}, u32[]{:S(2)}) %collective-permute-start) | collective-permute-done | bytes 524320 | tf_op jit(solution)/shard_map/ppermute | solution.py:17
  28.1 1.6 fusion.121
  29.8 14.9 %all-gather.7.cloned.1.call-done = f32[16,4,128,128]{3,2,1,0:T(8,128)} async-done(((f32[2,4,128,128]{3,2,1,0:T(8,128)}), f32[16,4,128,128]{3,2,1,0:T(8,128)}) %all-gather.7.cloned.1.call-update) | async-done | bytes 4194320 | tf_op jit(solution)/shard_map/all_gather | solution.py:76
  44.7 2.8 gather_fusion
  52.7 1.7 copy.150
  54.4 1.7 copy.196
  56.0 1.9 fusion.66
  57.9 2.0 copy.152
  59.9 2.1 fusion.77
  63.0 2.2 select_dynamic-update-slice_fusion.2
  66.9 2.8 select_dynamic-update-slice_fusion.1
  71.7 2.9 fusion.91
  75.5 1.8 copy.157
  77.4 2.1 reshape.911
  79.5 4.8 %multiply_reduce_fusion.1 = (f32[2]{0:T(128)S(1)}, f32[2,512,512]{2,1,0:T(8,128)}) fusion(f32[2,512,512]{2,1,0:T(8,128)S(1)} %reshape.911), kind=kOutput, calls=%fused_computation.38 | convolution fusion | flops 3222274048 | bytes 4194312 | tf_op jit(solution)/shard_map/sab,sbc->sac/dot_general | solution.py:89
  85.6 64.9 %pmax.14 = f32[]{:T(128)} all-reduce(f32[]{:T(128)} %reduce_max.18), channel_id=1, replica_groups=mesh['row'=8,'col'=16] {'row','col'}, use_global_device_ids=true, to_apply=%region_5.6 | all-reduce | flops 1 | bytes 8 | tf_op jit(solution)/shard_map/pmax | solution.py:93
  151.2 5.3 %fusion.29 = f32[2,512,512]{2,1,0:T(8,128)S(1)} fusion(f32[2,512,512]{2,1,0:T(8,128)} %get-tuple-element.289, f32[2,512,512]{2,1,0:T(8,128)S(1)} %reshape.911, f32[]{:T(128)S(6)} %mul.227, f32[512,512]{1,0:T(8,128)S(1)} %broadcast_select_fusion, f32[]{:T(128)S(6)} %div.33), kind=kOutput, calls=%fused_computation.33 | convolution fusion | flops 3223322624 | bytes 7340040 | tf_op jit(solution)/shard_map/sab,sbc->sac/dot_general | solution.py:54
  156.6 3.5 fusion.125
  160.1 3.7 fusion.26
  163.8 3.8 fusion.126
  167.6 3.7 fusion.23
  171.3 3.5 fusion.127
  174.8 3.7 fusion.20
  178.5 4.0 fusion.128
  182.5 3.7 fusion.17
  186.2 3.5 fusion.129
  189.8 1.9 fusion.35
  194.0 4.1 %collective-permute-start.3 = (f32[1,2,4,128,128]{3,4,1,2,0:T(8,128)S(1)}, f32[1,2,4,128,128]{3,4,1,2,0:T(8,128)}, u32[]{:S(2)}, u32[]{:S(2)}) collective-permute-start(f32[1,2,4,128,128]{3,4,1,2,0:T(8,128)S(1)} %broadcast_multiply_fusion.1), channel_id=1, source_target_pairs={{1,0},{2,1},{3,2},{4,3},{5,4},{6,5},{7,6},{8,7},{9,8},{10,9},{11,1... | collective-permute-start | bytes 1572872 | tf_op jit(solution)/shard_map/ppermute | solution.py:20
  198.9 10.6 %collective-permute-done.2 = f32[1,2,4,128,128]{3,4,1,2,0:T(8,128)} collective-permute-done((f32[1,2,4,128,128]{3,4,1,2,0:T(8,128)S(1)}, f32[1,2,4,128,128]{3,4,1,2,0:T(8,128)}, u32[]{:S(2)}, u32[]{:S(2)}) %collective-permute-start.2) | collective-permute-done | bytes 524320 | tf_op jit(solution)/shard_map/ppermute | solution.py:17
  209.5 1.6 slice_bitcast_fusion.4
  211.3 1.6 slice_bitcast_fusion.3
  213.0 1.6 fusion.97
  214.7 1.6 fusion.94
  216.3 3.0 copy.160
  219.3 2.2 gather_fusion.1
  222.3 1.9 fusion.114
  236.7 2.2 select_dynamic-update-slice_fusion
  240.7 1.9 fusion.90
  243.7 1.8 copy.185
  246.3 3.6 fusion.89
  249.9 1.6 fusion.82
  251.5 4.2 %copy.187 = f32[2,4,128,4,128]{4,3,2,1,0:T(4,128)} copy(f32[2,4,128,4,128]{4,2,0,3,1:T(8,128)} %fusion.82) | data formatting | bytes 4194304 | tf_op jit(solution)/shard_map/vmap()/scatter | solution.py:39
  255.7 2.1 reshape.924
  257.8 4.8 %multiply_reduce_fusion = (f32[2]{0:T(128)S(1)}, f32[2,512,512]{2,1,0:T(8,128)}) fusion(f32[2,512,512]{2,1,0:T(8,128)S(1)} %reshape.924), kind=kOutput, calls=%fused_computation.20 | convolution fusion | flops 3222274048 | bytes 4194312 | tf_op jit(solution)/shard_map/sab,sbc->sac/dot_general | solution.py:89
  263.2 64.9 %pmax.15 = f32[]{:T(128)} all-reduce(f32[]{:T(128)} %reduce_max.19), channel_id=1, replica_groups=mesh['row'=8,'col'=16] {'row','col'}, use_global_device_ids=true, to_apply=%region_8.9 | all-reduce | flops 1 | bytes 8 | tf_op jit(solution)/shard_map/pmax | solution.py:93
  328.8 5.3 %fusion.12 = f32[2,512,512]{2,1,0:T(8,128)S(1)} fusion(f32[2,512,512]{2,1,0:T(8,128)} %get-tuple-element.291, f32[2,512,512]{2,1,0:T(8,128)S(1)} %reshape.924, f32[]{:T(128)S(6)} %mul.251, f32[]{:T(128)S(6)} %div.34, f32[512,512]{1,0:T(8,128)S(1)} %broadcast_select_fusion), kind=kOutput, calls=%fused_computation.15 | convolution fusion | flops 3223322624 | bytes 7340040 | tf_op jit(solution)/shard_map/sab,sbc->sac/dot_general | solution.py:54
  334.2 3.5 fusion.130
  337.7 3.7 fusion.9
  341.4 4.0 fusion.131
  345.4 3.7 fusion.6
  349.1 3.5 fusion.132
  352.6 3.7 fusion.3
  356.3 3.7 fusion.133
  360.1 3.7 fusion
  363.8 3.5 fusion.134
  367.3 1.9 fusion.34
  371.1 4.5 %collective-permute-start.5 = (f32[1,2,4,128,128]{3,4,1,2,0:T(8,128)S(1)}, f32[1,2,4,128,128]{3,4,1,2,0:T(8,128)S(1)}, u32[]{:S(2)}, u32[]{:S(2)}) collective-permute-start(f32[1,2,4,128,128]{3,4,1,2,0:T(8,128)S(1)} %broadcast_multiply_fusion), channel_id=1, source_target_pairs={{1,0},{2,1},{3,2},{4,3},{5,4},{6,5},{7,6},{8,7},{9,8},{10,9},{11,1... | collective-permute-start | bytes 1572872 | tf_op jit(solution)/shard_map/ppermute | solution.py:20
  375.8 11.2 %collective-permute-done.4 = f32[1,2,4,128,128]{3,4,1,2,0:T(8,128)S(1)} collective-permute-done((f32[1,2,4,128,128]{3,4,1,2,0:T(8,128)S(1)}, f32[1,2,4,128,128]{3,4,1,2,0:T(8,128)S(1)}, u32[]{:S(2)}, u32[]{:S(2)}) %collective-permute-start.4) | collective-permute-done | bytes 524320 | tf_op jit(solution)/shard_map/ppermute | solution.py:17
  387.0 6.1 %all-gather.11.cloned.1.call-done = f32[16,2,128,128]{2,3,0,1:T(8,128)} async-done(((f32[2,2,128,128]{2,3,0,1:T(8,128)}), f32[16,2,128,128]{2,3,0,1:T(8,128)}) %all-gather.11.cloned.1.call-update) | async-done | bytes 2097168 | tf_op jit(solution)/shard_map/all_gather | solution.py:102
  393.1 1.9 copy.190
  (141 shorter events, 43.3 us)
Async XLA Ops:
  6.5 15.7 %copy-start.17 = (s32[5]{0:T(128)S(1)}, s32[5]{0:T(128)}, u32[]{:S(2)}) copy-start(s32[5]{0:T(128)} %constant.550.clone.1) | copy-start | bytes 64
  6.5 38.2 %all-gather.7.cloned.1.call-start = ((), (), s32[]{:S(2)}) async-start(), calls=%async_computation | async-start | bytes 4718592 | tf_op jit(solution)/shard_map/all_gather | solution.py:76
  7.3 209.0 %all-gather.9.cloned.1.call-start = ((), (), s32[]{:S(2)}) async-start(), calls=%async_computation.1 | async-start | bytes 2359296 | tf_op jit(solution)/shard_map/all_gather | solution.py:102
  8.6 18.7 %collective-permute-start = (f32[1,2,4,128,128]{3,4,1,2,0:T(8,128)S(1)}, f32[1,2,4,128,128]{3,4,1,2,0:T(8,128)S(1)}, u32[]{:S(2)}, u32[]{:S(2)}) collective-permute-start(f32[1,2,4,128,128]{3,4,1,2,0:T(8,128)S(1)} %bitcast.233), channel_id=1, source_target_pairs={{0,1},{1,2},{2,3},{3,4},{4,5},{5,6},{6,7},{7,8},{8,9},{9,10},{10,1... | collective-permute-start | bytes 1572872 | tf_op jit(solution)/shard_map/ppermute | solution.py:17
  10.7 17.3 %collective-permute-start.1 = (f32[1,2,4,128,128]{3,4,1,2,0:T(8,128)S(1)}, f32[1,2,4,128,128]{3,4,1,2,0:T(8,128)}, u32[]{:S(2)}, u32[]{:S(2)}) collective-permute-start(f32[1,2,4,128,128]{3,4,1,2,0:T(8,128)S(1)} %bitcast.234), channel_id=1, source_target_pairs={{1,0},{2,1},{3,2},{4,3},{5,4},{6,5},{7,6},{8,7},{9,8},{10,9},{11,1... | collective-permute-start | bytes 1572872 | tf_op jit(solution)/shard_map/ppermute | solution.py:20
  22.1 26.3 %copy-start = (f32[2,4,128,128]{3,2,1,0:T(8,128)S(1)}, f32[2,4,128,128]{3,2,1,0:T(8,128)}, u32[]{:S(2)}) copy-start(f32[2,4,128,128]{3,2,1,0:T(8,128)} %param.42) | copy-start | bytes 1572868
  27.3 0.9 copy-start.14
  47.5 4.0 %copy-start.7 = (f32[2,4,128,128]{3,2,1,0:T(8,128)}, f32[2,4,128,128]{3,2,1,0:T(8,128)S(1)}, u32[]{:S(2)}) copy-start(f32[2,4,128,128]{3,2,1,0:T(8,128)S(1)} %gather_fusion) | copy-start | bytes 1572868
  48.4 0.8 copy-start.3
  51.5 1.2 copy-start.10
  186.2 3.6 copy-start.4
  192.8 200.2 %all-gather.11.cloned.1.call-start = ((), (), s32[]{:S(2)}) async-start(), calls=%async_computation.2 | async-start | bytes 2359296 | tf_op jit(solution)/shard_map/all_gather | solution.py:102
  193.2 16.3 %collective-permute-start.2 = (f32[1,2,4,128,128]{3,4,1,2,0:T(8,128)S(1)}, f32[1,2,4,128,128]{3,4,1,2,0:T(8,128)}, u32[]{:S(2)}, u32[]{:S(2)}) collective-permute-start(f32[1,2,4,128,128]{3,4,1,2,0:T(8,128)S(1)} %broadcast_multiply_fusion.1), channel_id=1, source_target_pairs={{0,1},{1,2},{2,3},{3,4},{4,5},{5,6},{6,7},{7,8},{8,9},{9,10},{10,1... | collective-permute-start | bytes 1572872 | tf_op jit(solution)/shard_map/ppermute | solution.py:17
  194.0 17.3 %collective-permute-start.3 = (f32[1,2,4,128,128]{3,4,1,2,0:T(8,128)S(1)}, f32[1,2,4,128,128]{3,4,1,2,0:T(8,128)}, u32[]{:S(2)}, u32[]{:S(2)}) collective-permute-start(f32[1,2,4,128,128]{3,4,1,2,0:T(8,128)S(1)} %broadcast_multiply_fusion.1), channel_id=1, source_target_pairs={{1,0},{2,1},{3,2},{4,3},{5,4},{6,5},{7,6},{8,7},{9,8},{10,9},{11,1... | collective-permute-start | bytes 1572872 | tf_op jit(solution)/shard_map/ppermute | solution.py:20
  216.3 6.0 %copy-start.1 = (f32[2,4,128,128]{3,2,1,0:T(8,128)S(1)}, f32[2,4,128,128]{3,2,1,0:T(8,128)}, u32[]{:S(2)}) copy-start(f32[2,4,128,128]{3,2,1,0:T(8,128)} %param.42) | copy-start | bytes 1572868
  222.3 3.8 copy-start.6
  224.2 2.6 copy-start.11
  224.2 2.6 copy-start.12
  226.1 0.7 copy-start.13
  227.0 3.0 copy-start.9
  228.4 3.9 copy-start.15
  228.5 4.5 %copy-start.8 = (f32[2,4,128,128]{3,2,0,1:T(8,128)}, f32[2,4,128,128]{3,2,0,1:T(8,128)S(1)}, u32[]{:S(2)}) copy-start(f32[2,4,128,128]{3,2,0,1:T(8,128)S(1)} %broadcast_multiply_fusion.4) | copy-start | bytes 1572868
  233.1 1.1 copy-start.2
  243.7 1.8 copy-start.16
  363.8 3.6 copy-start.5
  370.7 16.2 %collective-permute-start.4 = (f32[1,2,4,128,128]{3,4,1,2,0:T(8,128)S(1)}, f32[1,2,4,128,128]{3,4,1,2,0:T(8,128)S(1)}, u32[]{:S(2)}, u32[]{:S(2)}) collective-permute-start(f32[1,2,4,128,128]{3,4,1,2,0:T(8,128)S(1)} %broadcast_multiply_fusion), channel_id=1, source_target_pairs={{0,1},{1,2},{2,3},{3,4},{4,5},{5,6},{6,7},{7,8},{8,9},{9,10},{10,1... | collective-permute-start | bytes 1572872 | tf_op jit(solution)/shard_map/ppermute | solution.py:17
  371.1 15.9 %collective-permute-start.5 = (f32[1,2,4,128,128]{3,4,1,2,0:T(8,128)S(1)}, f32[1,2,4,128,128]{3,4,1,2,0:T(8,128)S(1)}, u32[]{:S(2)}, u32[]{:S(2)}) collective-permute-start(f32[1,2,4,128,128]{3,4,1,2,0:T(8,128)S(1)} %broadcast_multiply_fusion), channel_id=1, source_target_pairs={{1,0},{2,1},{3,2},{4,3},{5,4},{6,5},{7,6},{8,7},{9,8},{10,9},{11,1... | collective-permute-start | bytes 1572872 | tf_op jit(solution)/shard_map/ppermute | solution.py:20
Sparse Core Ops, SparseCore 0:
  9.0 35.6 all-gather.6
  192.9 22.8 all-gather.8
  370.5 22.4 all-gather.10
where the time goes:
time: 411 us; the launch traced here: 403 us
  blocking collectives  130 us (32%)
  matrix products  90.4 us (22%)
  local copies, waits for them, and re-layouts  68.9 us (17%)
  waiting for transfers between devices  47.9 us (12%)
  other arithmetic  33.9 us (8%)
  starting transfers between devices  17 us (4%)
  between operations  15.6 us (4%)
    pmax x2, blocking collectives, per_device(): largest = lax.pmax(local_top, ('row', 'col'))  130 us
    dot_general x12, matrix products, sign_batch(): jnp.einsum('sab,sbc->sac', iterate, 1.5 * identity - 0.5 * square, precis...  44.1 us
    dot_general x10, matrix products, sign_batch(): jnp.einsum('sab,sbc->sac', iterate, iterate, precision=lax.Precision.HIGH...  36.6 us
    ppermute x3, waiting for transfers between devices, with_halo(): lax.ppermute(lax.slice_in_dim(block, block.shape[dim] - width, None, axis...  26.1 us
    scatter x6, other arithmetic, assemble(): matrix = matrix.at[0, :, position, :].set(column[position].T)  15.7 us
    all_gather x1, waiting for transfers between devices, per_device(): everyone = lax.all_gather(hamiltonian[None], 'row', axis=0, tiled=True)  14.9 us
    another operation x17, local copies, waits for them, and re-layouts  13.6 us
    ppermute x3, starting transfers between devices, with_halo(): lax.ppermute(lax.slice_in_dim(block, 0, width, axis=dim), axis, backward)  13.5 us
  transfers between devices with their start and end apart: 9, of which 5 were waited for; matrix products, arithmetic and copies ran while one was open for 5% of the time, Pallas kernels for 0%

commit v1 on v0

--- a/solution.py
+++ b/solution.py
@@ -6,6 +6,11 @@
 ITERS = 6
 STEPS = 2
 epsilon = 1e-06
+
+
+def tiled_gather(array, axis, dim):
+    copies = jnp.concatenate([array] * lax.axis_size(axis), axis=dim)
+    return lax.all_to_all(copies, axis, dim, dim, tiled=True)
 
 
 def with_halo(block, sides, width):
@@ -99,7 +104,7 @@
         right_dens = cycle_dens[2][:, 1]
         right_centre = cycle_dens[2][:, 0]
         sent_partner = jnp.stack((density_cols[:, 3], density_cols[:, 0]), 1)
-        everyone_dens = lax.all_gather(sent_partner[None], "row", axis=0, tiled=True)
+        everyone_dens = tiled_gather(sent_partner[None], "row", 0)
         partner_pair = everyone_dens[partner_row, slot_ids]
         partner_dens = partner_pair[:, 0]
         partner_centre = partner_pair[:, 1]

time: 411 us -> 424 us (1.032)
  starting transfers between devices: 17 us -> 26.1 us
    all_to_all x0 -> x2, starting transfers between devices: none -> 9.25 us  [tiled_gather(): return lax.all_to_all(copies, axis, dim, dim, tiled=True)]
    all_gather x2 -> x0, waiting for transfers between devices: 6.08 us -> none  [per_device(): lax.all_gather(sent_partner[None], 'row', axis=0, tiled=True)]
    all_to_all x0 -> x2, waiting for transfers between devices: none -> 5.92 us  [tiled_gather(): return lax.all_to_all(copies, axis, dim, dim, tiled=True)]
    all_gather x2 -> x0, local copies, waits for them, and re-layouts: 4.96 us -> none  [per_device(): lax.all_gather(sent_partner[None], 'row', axis=0, tiled=True)]
    another operation x17 -> x19, local copies, waits for them, and re-layouts: 13.6 us -> 13.8 us
  transfers between devices with their start and end apart: 9 -> 9, of which waited for: 5 -> 6; matrix products, arithmetic and copies ran while one was open for 5% -> 6% of each run, Pallas kernels for 0% -> 0%
where the time goes in v1:
time: 424 us; the launch traced here: 416 us
  blocking collectives  129 us (30%)
  matrix products  90.4 us (21%)
  local copies, waits for them, and re-layouts  69.9 us (16%)
  waiting for transfers between devices  49.2 us (12%)
  other arithmetic  34.9 us (8%)
  starting transfers between devices  26.1 us (6%)
  between operations  15.9 us (4%)
    pmax x2, blocking collectives, per_device(): largest = lax.pmax(local_top, ('row', 'col'))  129 us
    dot_general x12, matrix products, sign_batch(): jnp.einsum('sab,sbc->sac', iterate, 1.5 * identity - 0.5 * square, precis...  44.1 us
    dot_general x10, matrix products, sign_batch(): jnp.einsum('sab,sbc->sac', iterate, iterate, precision=lax.Precision.HIGH...  36.6 us
    ppermute x3, waiting for transfers between devices, with_halo(): lax.ppermute(lax.slice_in_dim(block, block.shape[dim] - width, None, axis...  27.6 us
    scatter x6, other arithmetic, assemble(): matrix = matrix.at[0, :, position, :].set(column[position].T)  15.6 us
    all_gather x1, waiting for transfers between devices, per_device(): everyone = lax.all_gather(hamiltonian[None], 'row', axis=0, tiled=True)  15 us
    ppermute x3, starting transfers between devices, with_halo(): lax.ppermute(lax.slice_in_dim(block, 0, width, axis=dim), axis, backward)  13.7 us
    another operation x17, local copies, waits for them, and re-layouts  13.5 us
  transfers between devices with their start and end apart: 9, of which 6 were waited for; matrix products, arithmetic and copies ran while one was open for 6% of the time, Pallas kernels for 0%

profile of v1, /device:TPU:1, one launch (start us, length us, event | category | flops | bytes accessed | tf_op | source)
XLA Modules:
  0.0 416.0 jit_solution(12331892346808710019)
XLA Ops:
  8.5 2.2 collective-permute-start
  10.7 5.0 %collective-permute-start.1 = (f32[1,2,4,128,128]{3,4,1,2,0:T(8,128)S(1)}, f32[1,2,4,128,128]{3,4,1,2,0:T(8,128)}, u32[]{:S(2)}, u32[]{:S(2)}) collective-permute-start(f32[1,2,4,128,128]{3,4,1,2,0:T(8,128)S(1)} %bitcast.230), channel_id=1, source_target_pairs={{1,0},{2,1},{3,2},{4,3},{5,4},{6,5},{7,6},{8,7},{9,8},{10,9},{11,1... | collective-permute-start | bytes 1572872 | tf_op jit(solution)/shard_map/ppermute | solution.py:25
  22.8 4.4 %collective-permute-done = f32[1,2,4,128,128]{3,4,1,2,0:T(8,128)S(1)} collective-permute-done((f32[1,2,4,128,128]{3,4,1,2,0:T(8,128)S(1)}, f32[1,2,4,128,128]{3,4,1,2,0:T(8,128)S(1)}, u32[]{:S(2)}, u32[]{:S(2)}) %collective-permute-start) | collective-permute-done | bytes 524320 | tf_op jit(solution)/shard_map/ppermute | solution.py:22
  28.1 1.6 fusion.121
  29.7 15.0 %all-gather.3.cloned.1.call-done = f32[16,4,128,128]{3,2,1,0:T(8,128)} async-done(((f32[2,4,128,128]{3,2,1,0:T(8,128)}), f32[16,4,128,128]{3,2,1,0:T(8,128)}) %all-gather.3.cloned.1.call-update) | async-done | bytes 4194320 | tf_op jit(solution)/shard_map/all_gather | solution.py:81
  44.7 2.8 gather_fusion
  52.7 1.7 copy.152
  54.4 1.7 copy.198
  56.0 1.9 fusion.66
  57.9 2.1 copy.154
  59.9 2.1 fusion.77
  63.0 2.2 select_dynamic-update-slice_fusion.2
  66.9 2.8 select_dynamic-update-slice_fusion.1
  71.7 2.9 fusion.91
  75.5 1.8 copy.159
  77.3 2.1 reshape.915
  79.4 4.9 %multiply_reduce_fusion.1 = (f32[2]{0:T(128)S(1)}, f32[2,512,512]{2,1,0:T(8,128)}) fusion(f32[2,512,512]{2,1,0:T(8,128)S(1)} %reshape.915), kind=kOutput, calls=%fused_computation.38 | convolution fusion | flops 3222274048 | bytes 4194312 | tf_op jit(solution)/shard_map/sab,sbc->sac/dot_general | solution.py:94
  85.6 64.9 %pmax.14 = f32[]{:T(128)} all-reduce(f32[]{:T(128)} %reduce_max.18), channel_id=1, replica_groups=mesh['row'=8,'col'=16] {'row','col'}, use_global_device_ids=true, to_apply=%region_5.6 | all-reduce | flops 1 | bytes 8 | tf_op jit(solution)/shard_map/pmax | solution.py:98
  151.2 5.3 %fusion.29 = f32[2,512,512]{2,1,0:T(8,128)S(1)} fusion(f32[2,512,512]{2,1,0:T(8,128)} %get-tuple-element.289, f32[2,512,512]{2,1,0:T(8,128)S(1)} %reshape.915, f32[]{:T(128)S(6)} %mul.227, f32[512,512]{1,0:T(8,128)S(1)} %broadcast_select_fusion, f32[]{:T(128)S(6)} %div.33), kind=kOutput, calls=%fused_computation.33 | convolution fusion | flops 3223322624 | bytes 7340040 | tf_op jit(solution)/shard_map/sab,sbc->sac/dot_general | solution.py:59
  156.6 3.5 fusion.125
  160.1 3.7 fusion.26
  163.8 3.8 fusion.126
  167.6 3.7 fusion.23
  171.3 3.5 fusion.127
  174.8 3.7 fusion.20
  178.5 4.0 fusion.128
  182.5 3.7 fusion.17
  186.2 3.5 fusion.129
  189.8 1.9 fusion.35
  193.8 4.9 %all-to-all-start = ((f32[8,2,2,128,128]{4,3,2,1,0:T(8,128)}), f32[8,2,2,128,128]{4,3,2,1,0:T(8,128)}, u32[]{:S(2)}, u32[]{:S(2)}) async-start(f32[8,2,2,128,128]{4,3,2,1,0:T(8,128)} %concatenate.61), calls=%async_computation | async-start | bytes 4194304 | tf_op jit(solution)/shard_map/all_to_all | solution.py:13
  200.8 3.9 collective-permute-start.3
  205.6 11.2 %collective-permute-done.2 = f32[1,2,4,128,128]{3,4,1,2,0:T(8,128)} collective-permute-done((f32[1,2,4,128,128]{3,4,1,2,0:T(8,128)}, f32[1,2,4,128,128]{3,4,1,2,0:T(8,128)}, u32[]{:S(2)}, u32[]{:S(2)}) %collective-permute-start.2) | collective-permute-done | bytes 524320 | tf_op jit(solution)/shard_map/ppermute | solution.py:22
  216.7 1.6 slice_bitcast_fusion.4
  218.5 1.6 slice_bitcast_fusion.3
  220.2 1.6 fusion.97
  221.9 1.6 fusion.94
  225.0 2.2 gather_fusion.1
  227.9 1.9 fusion.114
  242.3 2.2 select_dynamic-update-slice_fusion
  246.4 1.9 fusion.90
  249.3 1.8 copy.187
  251.9 3.6 fusion.89
  255.5 1.6 fusion.82
  257.1 4.3 %copy.189 = f32[2,4,128,4,128]{4,3,2,1,0:T(4,128)} copy(f32[2,4,128,4,128]{4,2,0,3,1:T(8,128)} %fusion.82) | data formatting | bytes 4194304 | tf_op jit(solution)/shard_map/vmap()/scatter | solution.py:44
  261.3 2.1 reshape.928
  263.4 4.9 %multiply_reduce_fusion = (f32[2]{0:T(128)S(1)}, f32[2,512,512]{2,1,0:T(8,128)}) fusion(f32[2,512,512]{2,1,0:T(8,128)S(1)} %reshape.928), kind=kOutput, calls=%fused_computation.20 | convolution fusion | flops 3222274048 | bytes 4194312 | tf_op jit(solution)/shard_map/sab,sbc->sac/dot_general | solution.py:94
  268.9 64.6 %pmax.15 = f32[]{:T(128)} all-reduce(f32[]{:T(128)} %reduce_max.19), channel_id=1, replica_groups=mesh['row'=8,'col'=16] {'row','col'}, use_global_device_ids=true, to_apply=%region_8.9 | all-reduce | flops 1 | bytes 8 | tf_op jit(solution)/shard_map/pmax | solution.py:98
  334.2 5.3 %fusion.12 = f32[2,512,512]{2,1,0:T(8,128)S(1)} fusion(f32[2,512,512]{2,1,0:T(8,128)} %get-tuple-element.291, f32[2,512,512]{2,1,0:T(8,128)S(1)} %reshape.928, f32[]{:T(128)S(6)} %mul.251, f32[]{:T(128)S(6)} %div.34, f32[512,512]{1,0:T(8,128)S(1)} %broadcast_select_fusion), kind=kOutput, calls=%fused_computation.15 | convolution fusion | flops 3223322624 | bytes 7340040 | tf_op jit(solution)/shard_map/sab,sbc->sac/dot_general | solution.py:59
  339.5 3.5 fusion.130
  343.1 3.7 fusion.9
  346.8 4.0 fusion.131
  350.7 3.7 fusion.6
  354.4 3.5 fusion.132
  358.0 3.7 fusion.3
  361.7 3.7 fusion.133
  365.4 3.7 fusion
  369.1 3.5 fusion.134
  372.7 1.9 fusion.34
  375.1 1.6 concatenate.62
  376.7 4.4 %all-to-all-start.1 = ((f32[8,2,2,128,128]{4,3,2,1,0:T(8,128)}), f32[8,2,2,128,128]{4,3,2,1,0:T(8,128)S(1)}, u32[]{:S(2)}, u32[]{:S(2)}) async-start(f32[8,2,2,128,128]{4,3,2,1,0:T(8,128)} %concatenate.62), calls=%async_computation.1 | async-start | bytes 4194304 | tf_op jit(solution)/shard_map/all_to_all | solution.py:13
  382.1 1.9 broadcast_multiply_fusion
  384.0 4.8 %collective-permute-start.5 = (f32[1,2,4,128,128]{3,4,1,2,0:T(8,128)}, f32[1,2,4,128,128]{3,4,1,2,0:T(8,128)}, u32[]{:S(2)}, u32[]{:S(2)}) collective-permute-start(f32[1,2,4,128,128]{3,4,1,2,0:T(8,128)} %broadcast_multiply_fusion), channel_id=1, source_target_pairs={{1,0},{2,1},{3,2},{4,3},{5,4},{6,5},{7,6},{8,7},{9,8},{10,9},{11,1... | collective-permute-start | bytes 1572872 | tf_op jit(solution)/shard_map/ppermute | solution.py:25
  389.0 12.0 %collective-permute-done.4 = f32[1,2,4,128,128]{3,4,1,2,0:T(8,128)} collective-permute-done((f32[1,2,4,128,128]{3,4,1,2,0:T(8,128)}, f32[1,2,4,128,128]{3,4,1,2,0:T(8,128)}, u32[]{:S(2)}, u32[]{:S(2)}) %collective-permute-start.4) | collective-permute-done | bytes 524320 | tf_op jit(solution)/shard_map/ppermute | solution.py:22
  402.9 4.4 %all-to-all-done.1 = f32[8,2,2,128,128]{4,3,2,1,0:T(8,128)S(1)} async-done(((f32[8,2,2,128,128]{4,3,2,1,0:T(8,128)}), f32[8,2,2,128,128]{4,3,2,1,0:T(8,128)S(1)}, u32[]{:S(2)}, u32[]{:S(2)}) %all-to-all-start.1) | async-done | bytes 2097184 | tf_op jit(solution)/shard_map/all_to_all | solution.py:13
  (141 shorter events, 51.0 us)
Async XLA Ops:
  6.5 15.6 %copy-start.17 = (s32[5]{0:T(128)S(1)}, s32[5]{0:T(128)}, u32[]{:S(2)}) copy-start(s32[5]{0:T(128)} %constant.550.clone.1) | copy-start | bytes 64
  6.5 38.2 %all-gather.3.cloned.1.call-start = ((), (), s32[]{:S(2)}) async-start(), calls=%async_computation.2 | async-start | bytes 4718592 | tf_op jit(solution)/shard_map/all_gather | solution.py:81
  8.5 18.7 %collective-permute-start = (f32[1,2,4,128,128]{3,4,1,2,0:T(8,128)S(1)}, f32[1,2,4,128,128]{3,4,1,2,0:T(8,128)S(1)}, u32[]{:S(2)}, u32[]{:S(2)}) collective-permute-start(f32[1,2,4,128,128]{3,4,1,2,0:T(8,128)S(1)} %bitcast.229), channel_id=1, source_target_pairs={{0,1},{1,2},{2,3},{3,4},{4,5},{5,6},{6,7},{7,8},{8,9},{9,10},{10,1... | collective-permute-start | bytes 1572872 | tf_op jit(solution)/shard_map/ppermute | solution.py:22
  10.7 17.3 %collective-permute-start.1 = (f32[1,2,4,128,128]{3,4,1,2,0:T(8,128)S(1)}, f32[1,2,4,128,128]{3,4,1,2,0:T(8,128)}, u32[]{:S(2)}, u32[]{:S(2)}) collective-permute-start(f32[1,2,4,128,128]{3,4,1,2,0:T(8,128)S(1)} %bitcast.230), channel_id=1, source_target_pairs={{1,0},{2,1},{3,2},{4,3},{5,4},{6,5},{7,6},{8,7},{9,8},{10,9},{11,1... | collective-permute-start | bytes 1572872 | tf_op jit(solution)/shard_map/ppermute | solution.py:25
  22.0 26.3 %copy-start = (f32[2,4,128,128]{3,2,1,0:T(8,128)S(1)}, f32[2,4,128,128]{3,2,1,0:T(8,128)}, u32[]{:S(2)}) copy-start(f32[2,4,128,128]{3,2,1,0:T(8,128)} %param.42) | copy-start | bytes 1572868
  27.2 0.9 copy-start.14
  47.5 4.0 copy-start.7
  48.4 0.8 copy-start.3
  51.5 1.2 copy-start.10
  186.2 3.6 copy-start.4
  193.8 31.2 %all-to-all-start = ((f32[8,2,2,128,128]{4,3,2,1,0:T(8,128)}), f32[8,2,2,128,128]{4,3,2,1,0:T(8,128)}, u32[]{:S(2)}, u32[]{:S(2)}) async-start(f32[8,2,2,128,128]{4,3,2,1,0:T(8,128)} %concatenate.61), calls=%async_computation | async-start | bytes 4194304 | tf_op jit(solution)/shard_map/all_to_all | solution.py:13
  199.7 17.0 %collective-permute-start.2 = (f32[1,2,4,128,128]{3,4,1,2,0:T(8,128)}, f32[1,2,4,128,128]{3,4,1,2,0:T(8,128)}, u32[]{:S(2)}, u32[]{:S(2)}) collective-permute-start(f32[1,2,4,128,128]{3,4,1,2,0:T(8,128)} %broadcast_multiply_fusion.1), channel_id=1, source_target_pairs={{0,1},{1,2},{2,3},{3,4},{4,5},{5,6},{6,7},{7,8},{8,9},{9,10},{10,1... | collective-permute-start | bytes 1572872 | tf_op jit(solution)/shard_map/ppermute | solution.py:22
  200.8 17.7 %collective-permute-start.3 = (f32[1,2,4,128,128]{3,4,1,2,0:T(8,128)}, f32[1,2,4,128,128]{3,4,1,2,0:T(8,128)}, u32[]{:S(2)}, u32[]{:S(2)}) collective-permute-start(f32[1,2,4,128,128]{3,4,1,2,0:T(8,128)} %broadcast_multiply_fusion.1), channel_id=1, source_target_pairs={{1,0},{2,1},{3,2},{4,3},{5,4},{6,5},{7,6},{8,7},{9,8},{10,9},{11,1... | collective-permute-start | bytes 1572872 | tf_op jit(solution)/shard_map/ppermute | solution.py:25
  205.6 22.4 %copy-start.1 = (f32[2,4,128,128]{3,2,1,0:T(8,128)S(1)}, f32[2,4,128,128]{3,2,1,0:T(8,128)}, u32[]{:S(2)}) copy-start(f32[2,4,128,128]{3,2,1,0:T(8,128)} %param.42) | copy-start | bytes 1572868
  227.9 3.8 copy-start.6
  229.9 2.6 copy-start.11
  229.9 2.6 copy-start.12
  231.8 0.7 copy-start.13
  232.7 3.0 copy-start.9
  234.1 3.8 copy-start.15
  234.2 4.5 %copy-start.8 = (f32[2,4,128,128]{3,2,0,1:T(8,128)}, f32[2,4,128,128]{3,2,0,1:T(8,128)S(1)}, u32[]{:S(2)}) copy-start(f32[2,4,128,128]{3,2,0,1:T(8,128)S(1)} %broadcast_multiply_fusion.4) | copy-start | bytes 1572868
  238.7 1.1 copy-start.2
  249.3 1.8 copy-start.16
  369.1 3.6 copy-start.5
  376.7 30.6 %all-to-all-start.1 = ((f32[8,2,2,128,128]{4,3,2,1,0:T(8,128)}), f32[8,2,2,128,128]{4,3,2,1,0:T(8,128)S(1)}, u32[]{:S(2)}, u32[]{:S(2)}) async-start(f32[8,2,2,128,128]{4,3,2,1,0:T(8,128)} %concatenate.62), calls=%async_computation.1 | async-start | bytes 4194304 | tf_op jit(solution)/shard_map/all_to_all | solution.py:13
  384.0 17.0 %collective-permute-start.4 = (f32[1,2,4,128,128]{3,4,1,2,0:T(8,128)}, f32[1,2,4,128,128]{3,4,1,2,0:T(8,128)}, u32[]{:S(2)}, u32[]{:S(2)}) collective-permute-start(f32[1,2,4,128,128]{3,4,1,2,0:T(8,128)} %broadcast_multiply_fusion), channel_id=1, source_target_pairs={{0,1},{1,2},{2,3},{3,4},{4,5},{5,6},{6,7},{7,8},{8,9},{9,10},{10,1... | collective-permute-start | bytes 1572872 | tf_op jit(solution)/shard_map/ppermute | solution.py:22
  384.0 17.9 %collective-permute-start.5 = (f32[1,2,4,128,128]{3,4,1,2,0:T(8,128)}, f32[1,2,4,128,128]{3,4,1,2,0:T(8,128)}, u32[]{:S(2)}, u32[]{:S(2)}) collective-permute-start(f32[1,2,4,128,128]{3,4,1,2,0:T(8,128)} %broadcast_multiply_fusion), channel_id=1, source_target_pairs={{1,0},{2,1},{3,2},{4,3},{5,4},{6,5},{7,6},{8,7},{9,8},{10,9},{11,1... | collective-permute-start | bytes 1572872 | tf_op jit(solution)/shard_map/ppermute | solution.py:25
Sparse Core Ops, SparseCore 0:
  9.0 35.6 all-gather.2
